TPU v7x, 256 devices: a whole 4x4x8 slice. The times are simulated.
256 devices in a mesh: video: 8 (over z), seq: 32 (over x, y, core).
Axes of the slice: x: 4, y: 4, z: 8, core: 2. Of those that a mesh axis runs over, the one named last changes fastest.
Arguments:
- queries: bfloat16 [65536, 5120], P(('video', 'seq')), parts along dimension 0, may hold values from -8 to 8
- keys: bfloat16 [65536, 5120], P(('video', 'seq')), parts along dimension 0, may hold values from -8 to 8
- values: bfloat16 [65536, 5120], P(('video', 'seq')), parts along dimension 0, may hold values from -6 to 6
- temporal_heads: int32 [4], replicated, may hold values from 0 to 39, as said below
- spatial_mask: int32 [32, 4, 4], P('seq'), may hold values 0 or 1
- temporal_mask: int32 [32, 32], replicated, may hold values 0 or 1
Outputs:
- attended: bfloat16 [65536, 5120], P(('video', 'seq')), parts along dimension 0
There are 8 independent parts, one for each index of `video`. A program takes and returns all parts, laid end to end along the dimension named above; an argument that names none is the same for every part. Nothing has to cross between parts.
Inputs may be any that keep to these rules, and one draw needn't show every extreme that they name: `temporal_heads`: 4 different head numbers in rising order; the last one is always 40 - 1.
All inputs are finite; a program needn't handle non-finite values. No bound on the sum of `spatial_mask` on one device may be relied on, other than what follows from the above.
Results may differ from a plain program's by a relative error of at most 0.0049.
Values may be sent and summed in bfloat16 or wider, within the bound.
A program may use at most 64 MiB of HBM per device.

v0:
```python
import jax
import jax.numpy as jnp
from jax import lax
from jax.sharding import PartitionSpec as P

HEADS = 40
HD = 128
TEMPORAL = 4
SPATIAL = 36
BLK = 64
PG = 8


def attend(query, key, value, allowed):
    scores = jnp.einsum("qhd,khd->hqk", query, key, preferred_element_type=jnp.float32) * HD ** (
        -0.5
    )
    scores = jnp.where(allowed[None], scores, -1e30)
    top = jnp.max(scores, axis=2, keepdims=True)
    expo = jnp.exp(scores - top)
    probs = (expo / jnp.sum(expo, axis=2, keepdims=True)).astype(jnp.bfloat16)
    mixed = jnp.einsum("hqk,khd->qhd", probs, value, preferred_element_type=jnp.float32)
    return mixed.astype(jnp.bfloat16)


def on_device(queries, keys, values, temporal_heads, spatial_mask, temporal_mask):
    frames = lax.axis_size("seq")
    tok_rows = queries.shape[0]
    span = tok_rows // frames
    marks = jnp.any(
        jnp.arange(HEADS, dtype=jnp.int32)[:, None] == temporal_heads[None, :], axis=1
    ).astype(jnp.int32)
    order = jnp.argsort(marks, stable=True)
    inverse = jnp.argsort(order)

    def arrange(array):
        return jnp.take(array.reshape(tok_rows, HEADS, HD), order, axis=1)

    q_all, k_all, v_all = (arrange(queries), arrange(keys), arrange(values))
    blocks = tok_rows // BLK
    allow = (spatial_mask[0] != 0) | jnp.eye(blocks, dtype=bool)
    allow = jnp.broadcast_to(allow[:, None, :, None], (blocks, BLK, blocks, BLK)).reshape(
        tok_rows, tok_rows
    )
    spatial_out = attend(q_all[:, :SPATIAL], k_all[:, :SPATIAL], v_all[:, :SPATIAL], allow)
    frame_allow = (temporal_mask != 0) | jnp.eye(frames, dtype=bool)
    frame_allow = jnp.broadcast_to(frame_allow[:, None, :, None], (frames, PG, frames, PG)).reshape(
        frames * PG, frames * PG
    )
    groups = span // PG

    def outgoing(array):
        return array[:, SPATIAL:].reshape(frames, span, TEMPORAL, HD)

    q_pos = lax.all_to_all(outgoing(q_all), "seq", split_axis=0, concat_axis=0, tiled=True)
    k_pos = lax.all_to_all(outgoing(k_all), "seq", split_axis=0, concat_axis=0, tiled=True)
    v_pos = lax.all_to_all(outgoing(v_all), "seq", split_axis=0, concat_axis=0, tiled=True)
    width = q_pos.shape[2]

    def regroup(array):
        return jnp.transpose(array.reshape(frames, groups, PG, width, HD), (1, 0, 2, 3, 4)).reshape(
            groups, frames * PG, width, HD
        )

    q_grp = regroup(q_pos)
    k_grp = regroup(k_pos)
    v_grp = regroup(v_pos)
    scores = jnp.einsum(
        "gqhd,gkhd->ghqk", q_grp, k_grp, preferred_element_type=jnp.float32
    ) * HD ** (-0.5)
    scores = jnp.where(frame_allow[None, None], scores, -1e30)
    top = jnp.max(scores, axis=3, keepdims=True)
    expo = jnp.exp(scores - top)
    probs = (expo / jnp.sum(expo, axis=3, keepdims=True)).astype(jnp.bfloat16)
    mixed = jnp.einsum("ghqk,gkhd->gqhd", probs, v_grp, preferred_element_type=jnp.float32).astype(
        jnp.bfloat16
    )
    mixed = jnp.transpose(mixed.reshape(groups, frames, PG, width, HD), (1, 0, 2, 3, 4)).reshape(
        frames, span, width, HD
    )
    returned = mixed
    returned = lax.all_to_all(returned, "seq", split_axis=0, concat_axis=0, tiled=True)
    temporal_out = returned.reshape(tok_rows, TEMPORAL, HD)
    joined = jnp.concatenate([spatial_out, temporal_out], axis=1)
    joined = jnp.take(joined, inverse, axis=1)
    return joined.reshape(tok_rows, HEADS * HD)


def solution(mesh):
    placed = (
        P(("video", "seq"), None),
        P(("video", "seq"), None),
        P(("video", "seq"), None),
        P(),
        P("seq", None, None),
        P(),
    )
    return jax.shard_map(
        on_device, mesh=mesh, in_specs=placed, out_specs=P(("video", "seq"), None), check_vma=False
    )
```

profile of v0, /device:TPU:1, one launch (start us, length us, event | category | flops | bytes accessed | tf_op | source)
XLA Modules:
  0.0 130.8 jit_solution(13842758865024556322)
XLA Ops:
  0.8 2.0 %sort.34 = (s32[40]{0:T(128)}, s32[40]{0:T(128)S(1)}) sort(s32[40]{0:T(128)S(1)} %convert_element_type.25, s32[40]{0:T(128)S(1)} %iota.36), dimensions={0}, to_apply=%region_1.0 | sort | flops 240 | bytes 640 | tf_op jit(solution)/shard_map/jit(argsort)/sort | solution.py:33
  2.8 4.4 %copy.66 = bf16[256,5120]{0,1:T(8,128)(2,1)} copy(bf16[256,5120]{1,0:T(8,128)(2,1)} %param.8) | data formatting | bytes 5242880 | tf_op args[0]
  7.2 3.2 %copy.67 = bf16[256,40,128]{2,0,1:T(8,128)(2,1)S(1)} copy(bf16[256,40,128]{0,2,1:T(8,128)(2,1)} %bitcast.57) | data formatting | bytes 5242880 | tf_op jit(solution)/shard_map/reshape | solution.py:37
  10.4 4.4 %copy.68 = bf16[256,5120]{0,1:T(8,128)(2,1)} copy(bf16[256,5120]{1,0:T(8,128)(2,1)} %param.9) | data formatting | bytes 5242880 | tf_op args[1]
  14.8 4.4 %copy.69 = bf16[256,40,128]{2,0,1:T(8,128)(2,1)} copy(bf16[256,40,128]{0,2,1:T(8,128)(2,1)} %bitcast.58) | data formatting | bytes 5242880 | tf_op jit(solution)/shard_map/reshape | solution.py:37
  19.2 2.5 %gather_fusion.1 = bf16[40,256,128]{2,1,0:T(8,128)(2,1)} fusion(bf16[256,40,128]{2,0,1:T(8,128)(2,1)S(1)} %copy.67, s32[1024]{0:T(1024)S(1)} %pad_clamp_fusion.1), kind=kCustom, calls=%fused_computation.1.clone | custom fusion | bytes 5243040 | tf_op jit(solution)/shard_map/jit(_take)/gather | solution.py:37
  21.7 4.5 %gather_fusion.2 = bf16[40,256,128]{2,1,0:T(8,128)(2,1)} fusion(bf16[256,40,128]{2,0,1:T(8,128)(2,1)} %copy.69, s32[1024]{0:T(1024)S(1)} %pad_clamp_fusion.1), kind=kCustom, calls=%fused_computation.2.clone | custom fusion | bytes 5243040 | tf_op jit(solution)/shard_map/jit(_take)/gather | solution.py:37
  26.2 3.8 %select_bitcast_fusion.1 = (bf16[256,40,128]{2,0,1:T(8,128)(2,1)}, bf16[256,40,128]{2,0,1:T(8,128)(2,1)S(1)}) fusion(bf16[40,256,128]{2,1,0:T(8,128)(2,1)S(1)} %copy-done, pred[40]{0:T(512)(128)(4,1)S(1)} %compare_and_fusion.1, bf16[40,256,128]{2,1,0:T(8,128)(2,1)} %gather_fusion.2), kind=kLoop, calls=%fused_computation.16 | loop fusion | flops 2621440 | bytes 10485800 | tf_op jit(solution)/shard_map/jit(_take)/select_n | solution.py:37
  29.9 1.5 %copy-done.3 = bf16[256,40,128]{2,0,1:T(8,128)(2,1)} copy-done((bf16[256,40,128]{2,0,1:T(8,128)(2,1)}, bf16[256,40,128]{2,0,1:T(8,128)(2,1)S(1)}, u32[]{:S(2)}) %copy-start.3) | copy-done | bytes 2621464
  32.2 8.6 %all-to-all-start.2 = ((bf16[32,8,4,128]{3,1,2,0:T(8,128)(2,1)}), bf16[32,8,4,128]{3,1,2,0:T(8,128)(2,1)S(1)}, u32[]{:S(2)}, u32[]{:S(2)}) async-start(bf16[32,8,4,128]{3,1,2,0:T(8,128)(2,1)} %copy.77), calls=%async_computation.2 | async-start | bytes 524288 | tf_op jit(solution)/shard_map/all_to_all | solution.py:56
  40.8 4.4 %copy.62 = bf16[256,5120]{0,1:T(8,128)(2,1)} copy(bf16[256,5120]{1,0:T(8,128)(2,1)} %param.10) | data formatting | bytes 5242880 | tf_op args[2]
  45.2 3.2 %copy.63 = bf16[256,40,128]{2,0,1:T(8,128)(2,1)S(1)} copy(bf16[256,40,128]{0,2,1:T(8,128)(2,1)} %bitcast.59) | data formatting | bytes 5242880 | tf_op jit(solution)/shard_map/reshape | solution.py:37
  48.4 2.6 %gather_fusion = bf16[40,256,128]{2,1,0:T(8,128)(2,1)} fusion(bf16[256,40,128]{2,0,1:T(8,128)(2,1)S(1)} %copy.63, s32[1024]{0:T(1024)S(1)} %pad_clamp_fusion.1), kind=kCustom, calls=%fused_computation.clone | custom fusion | bytes 5243040 | tf_op jit(solution)/shard_map/jit(_take)/gather | solution.py:37
  51.0 3.0 %copy.64 = bf16[40,256,128]{1,2,0:T(8,128)(2,1)S(1)} copy(bf16[40,256,128]{2,1,0:T(8,128)(2,1)} %gather_fusion) | data formatting | bytes 5242880 | tf_op jit(solution)/shard_map/jit(_take)/gather | solution.py:37
  54.0 1.8 %select_bitcast_fusion.2 = bf16[256,40,128]{0,2,1:T(8,128)(2,1)} fusion(bf16[40,256,128]{1,2,0:T(8,128)(2,1)S(1)} %copy.64, pred[40]{0:T(512)(128)(4,1)S(1)} %compare_and_fusion.1), kind=kLoop, calls=%fused_computation.17 | loop fusion | flops 1310720 | bytes 5242920 | tf_op jit(solution)/shard_map/jit(_take)/select_n | solution.py:37
  55.8 0.9 copy-done.2
  57.5 5.0 %fusion.7 = f32[36,256,256]{1,2,0:T(8,128)} fusion(bf16[256,40,128]{2,0,1:T(8,128)(2,1)S(1)} %copy-done.2, bf16[256,40,128]{2,0,1:T(8,128)(2,1)S(1)} %copy-done.4), kind=kOutput, calls=%fused_computation.19 | convolution fusion | flops 603979776 | bytes 14417920 | tf_op jit(solution)/shard_map/qhd,khd->hqk/dot_general | solution.py:15
  63.0 10.1 %fusion.40 = (f32[36,256]{1,0:T(8,128)S(1)}, f32[36,256,256]{1,2,0:T(8,128)S(1)}) fusion(f32[36,256,256]{1,2,0:T(8,128)} %fusion.7, pred[256,256]{0,1:T(8,128)(4,1)S(1)} %broadcast_in_dim.56), kind=kOutput, calls=%fused_computation.56 | output fusion | flops 14156031 | bytes 18976768 | tf_op jit(solution)/shard_map/sub | solution.py:20
  73.1 2.4 %convert_bitcast_fusion = bf16[256,36,128]{0,2,1:T(8,128)(2,1)} fusion(bf16[256,40,128]{0,2,1:T(8,128)(2,1)S(1)} %copy-done.1, f32[36,256,256]{1,2,0:T(8,128)S(1)} %get-tuple-element.15, f32[36,256]{1,0:T(8,128)S(1)} %get-tuple-element.14), kind=kOutput, calls=%fused_computation.21 | convolution fusion | flops 609878016 | bytes 14454784 | tf_op jit(solution)/shard_map/hqk,khd->qhd/dot_general | solution.py:22
  75.6 1.0 slice_bitcast_fusion.1
  77.3 7.4 %all-to-all-start.1 = ((bf16[32,8,4,128]{3,1,2,0:T(8,128)(2,1)}), bf16[32,8,4,128]{3,1,2,0:T(8,128)(2,1)S(1)}, u32[]{:S(2)}, u32[]{:S(2)}) async-start(bf16[32,8,4,128]{3,1,2,0:T(8,128)(2,1)} %copy.75), calls=%async_computation.1 | async-start | bytes 524288 | tf_op jit(solution)/shard_map/all_to_all | solution.py:55
  85.1 2.9 %broadcast_in_dim.60 = pred[256,256]{1,0:T(8,128)(4,1)S(1)} reshape(pred[32,8,32,8]{3,2,1,0:T(8,128)(4,1)S(1)} %broadcast_in_dim.59) | data formatting | bytes 131072 | tf_op jit(solution)/shard_map/jit(_where)/broadcast_in_dim | solution.py:71
  89.1 2.0 %sort.35 = (s32[40]{0:T(128)}, s32[40]{0:T(128)S(1)}) sort(s32[40]{0:T(128)S(1)} %get-tuple-element.8, s32[40]{0:T(128)S(1)} %iota.41), dimensions={0}, to_apply=%region_6.8 | sort | flops 240 | bytes 640 | tf_op jit(solution)/shard_map/jit(argsort)/sort | solution.py:34
  91.1 2.5 %all-to-all-done.1 = bf16[32,8,4,128]{3,1,2,0:T(8,128)(2,1)S(1)} async-done(((bf16[32,8,4,128]{3,1,2,0:T(8,128)(2,1)}), bf16[32,8,4,128]{3,1,2,0:T(8,128)(2,1)S(1)}, u32[]{:S(2)}, u32[]{:S(2)}) %all-to-all-start.1) | async-done | bytes 262176 | tf_op jit(solution)/shard_map/all_to_all | solution.py:55
  93.7 4.9 %all-to-all-start = ((bf16[32,8,4,128]{3,1,2,0:T(8,128)(2,1)}), bf16[32,8,4,128]{3,1,2,0:T(8,128)(2,1)S(1)}, u32[]{:S(2)}, u32[]{:S(2)}) async-start(bf16[32,8,4,128]{3,1,2,0:T(8,128)(2,1)} %copy.72), calls=%async_computation | async-start | bytes 524288 | tf_op jit(solution)/shard_map/all_to_all | solution.py:57
  99.0 8.5 %all-to-all-done = bf16[32,8,4,128]{3,1,2,0:T(8,128)(2,1)S(1)} async-done(((bf16[32,8,4,128]{3,1,2,0:T(8,128)(2,1)}), bf16[32,8,4,128]{3,1,2,0:T(8,128)(2,1)S(1)}, u32[]{:S(2)}, u32[]{:S(2)}) %all-to-all-start) | async-done | bytes 262176 | tf_op jit(solution)/shard_map/all_to_all | solution.py:57
  108.7 3.7 %all-to-all-start.3 = ((bf16[32,8,4,128]{3,1,2,0:T(8,128)(2,1)}), bf16[32,8,4,128]{3,1,2,0:T(8,128)(2,1)S(1)}, u32[]{:S(2)}, u32[]{:S(2)}) async-start(bf16[32,8,4,128]{3,1,2,0:T(8,128)(2,1)} %copy.82), calls=%async_computation.3 | async-start | bytes 524288 | tf_op jit(solution)/shard_map/all_to_all | solution.py:82
  112.5 9.0 %all-to-all-done.3 = bf16[32,8,4,128]{3,1,2,0:T(8,128)(2,1)S(1)} async-done(((bf16[32,8,4,128]{3,1,2,0:T(8,128)(2,1)}), bf16[32,8,4,128]{3,1,2,0:T(8,128)(2,1)S(1)}, u32[]{:S(2)}, u32[]{:S(2)}) %all-to-all-start.3) | async-done | bytes 262176 | tf_op jit(solution)/shard_map/all_to_all | solution.py:82
  121.7 1.9 %pad_maximum_fusion = bf16[256,40,128]{0,2,1:T(8,128)(2,1)S(1)} fusion(bf16[256,4,128]{0,2,1:T(8,128)(2,1)S(1)} %copy.84, bf16[256,36,128]{0,2,1:T(8,128)(2,1)} %convert_bitcast_fusion), kind=kLoop, calls=%fused_computation.14 | loop fusion | flops 1310720 | bytes 5242880 | tf_op jit(solution)/shard_map/concatenate | solution.py:84
  123.6 2.4 %gather_fusion.3 = bf16[40,256,128]{1,2,0:T(8,128)(2,1)} fusion(bf16[256,40,128]{0,2,1:T(8,128)(2,1)S(1)} %pad_maximum_fusion, s32[1024]{0:T(1024)S(1)} %pad_clamp_fusion), kind=kCustom, calls=%fused_computation.3.clone | custom fusion | bytes 5243040 | tf_op jit(solution)/shard_map/jit(_take)/gather | solution.py:85
  126.0 2.0 %broadcast_select_fusion = bf16[40,256,128]{1,2,0:T(8,128)(2,1)S(1)} fusion(bf16[40,256,128]{1,2,0:T(8,128)(2,1)} %gather_fusion.3, pred[40]{0:T(512)(128)(4,1)S(1)} %compare_and_fusion), kind=kLoop, calls=%fused_computation.18 | loop fusion | flops 1310720 | bytes 5242920 | tf_op jit(solution)/shard_map/jit(_take)/select_n | solution.py:85
  128.0 2.8 %copy.85 = bf16[256,5120]{1,0:T(8,128)(2,1)} copy(bf16[256,5120]{0,1:T(8,128)(2,1)S(1)} %bitcast.56) | data formatting | bytes 5242880 | tf_op jit(solution)/shard_map/reshape | solution.py:86
  (43 shorter events, 7.0 us)
Async XLA Ops:
  21.7 4.5 %copy-start = (bf16[40,256,128]{2,1,0:T(8,128)(2,1)S(1)}, bf16[40,256,128]{2,1,0:T(8,128)(2,1)}, u32[]{:S(2)}) copy-start(bf16[40,256,128]{2,1,0:T(8,128)(2,1)} %gather_fusion.1) | copy-start | bytes 7864324
  29.9 1.5 %copy-start.3 = (bf16[256,40,128]{2,0,1:T(8,128)(2,1)}, bf16[256,40,128]{2,0,1:T(8,128)(2,1)S(1)}, u32[]{:S(2)}) copy-start(bf16[256,40,128]{2,0,1:T(8,128)(2,1)S(1)} %get-tuple-element.11) | copy-start | bytes 7864324
  32.2 45.1 %all-to-all-start.2 = ((bf16[32,8,4,128]{3,1,2,0:T(8,128)(2,1)}), bf16[32,8,4,128]{3,1,2,0:T(8,128)(2,1)S(1)}, u32[]{:S(2)}, u32[]{:S(2)}) async-start(bf16[32,8,4,128]{3,1,2,0:T(8,128)(2,1)} %copy.77), calls=%async_computation.2 | async-start | bytes 524288 | tf_op jit(solution)/shard_map/all_to_all | solution.py:56
  54.0 2.7 %copy-start.2 = (bf16[256,40,128]{2,0,1:T(8,128)(2,1)S(1)}, bf16[256,40,128]{2,0,1:T(8,128)(2,1)}, u32[]{:S(2)}) copy-start(bf16[256,40,128]{2,0,1:T(8,128)(2,1)} %get-tuple-element.10) | copy-start | bytes 7864324
  54.0 3.5 %copy-start.4 = (bf16[256,40,128]{2,0,1:T(8,128)(2,1)S(1)}, bf16[256,40,128]{2,0,1:T(8,128)(2,1)}, u32[]{:S(2)}) copy-start(bf16[256,40,128]{2,0,1:T(8,128)(2,1)} %copy-done.3) | copy-start | bytes 7864324
  57.5 5.0 %copy-start.6 = (s32[1,4,4]{2,1,0:T(4,128)S(1)}, s32[1,4,4]{2,1,0:T(4,128)}, u32[]{:S(2)}) copy-start(s32[1,4,4]{2,1,0:T(4,128)} %param.12) | copy-start | bytes 196
  63.0 10.1 %copy-start.1 = (bf16[256,40,128]{0,2,1:T(8,128)(2,1)S(1)}, bf16[256,40,128]{0,2,1:T(8,128)(2,1)}, u32[]{:S(2)}) copy-start(bf16[256,40,128]{0,2,1:T(8,128)(2,1)} %select_bitcast_fusion.2) | copy-start | bytes 7864324
  73.1 11.6 %copy-start.5 = (s32[32,32]{1,0:T(8,128)S(1)}, s32[32,32]{1,0:T(8,128)}, u32[]{:S(2)}) copy-start(s32[32,32]{1,0:T(8,128)} %param.13) | copy-start | bytes 12292
  75.6 12.6 %slice-start = ((bf16[256,40,128]{0,2,1:T(8,128)(2,1)}), bf16[256,4,128]{0,2,1:T(8,128)(2,1)S(1)}, s32[]{:S(2)}) async-start(bf16[256,40,128]{0,2,1:T(8,128)(2,1)} %select_bitcast_fusion.2), calls=%async_computation.4 | async-start | bytes 524288 | tf_op jit(solution)/shard_map/slice | solution.py:53
  77.3 16.3 %all-to-all-start.1 = ((bf16[32,8,4,128]{3,1,2,0:T(8,128)(2,1)}), bf16[32,8,4,128]{3,1,2,0:T(8,128)(2,1)S(1)}, u32[]{:S(2)}, u32[]{:S(2)}) async-start(bf16[32,8,4,128]{3,1,2,0:T(8,128)(2,1)} %copy.75), calls=%async_computation.1 | async-start | bytes 524288 | tf_op jit(solution)/shard_map/all_to_all | solution.py:55
  93.7 13.8 %all-to-all-start = ((bf16[32,8,4,128]{3,1,2,0:T(8,128)(2,1)}), bf16[32,8,4,128]{3,1,2,0:T(8,128)(2,1)S(1)}, u32[]{:S(2)}, u32[]{:S(2)}) async-start(bf16[32,8,4,128]{3,1,2,0:T(8,128)(2,1)} %copy.72), calls=%async_computation | async-start | bytes 524288 | tf_op jit(solution)/shard_map/all_to_all | solution.py:57
  108.7 12.8 %all-to-all-start.3 = ((bf16[32,8,4,128]{3,1,2,0:T(8,128)(2,1)}), bf16[32,8,4,128]{3,1,2,0:T(8,128)(2,1)S(1)}, u32[]{:S(2)}, u32[]{:S(2)}) async-start(bf16[32,8,4,128]{3,1,2,0:T(8,128)(2,1)} %copy.82), calls=%async_computation.3 | async-start | bytes 524288 | tf_op jit(solution)/shard_map/all_to_all | solution.py:82
where the time goes:
time: 132 us; the launch traced here: 131 us
  local copies, waits for them, and re-layouts  53.3 us (40%)
  starting transfers between devices  24.5 us (19%)
  other arithmetic  24.4 us (18%)
  waiting for transfers between devices  20 us (15%)
  matrix products  8.21 us (6%)
    unnamed x17, local copies, waits for them, and re-layouts  16.4 us
    gather x4, local copies, waits for them, and re-layouts, arrange(): return jnp.take(array.reshape(tok_rows, HEADS, HD), order, axis=1)  12.5 us
    reshape x3, local copies, waits for them, and re-layouts, arrange(): return jnp.take(array.reshape(tok_rows, HEADS, HD), order, axis=1)  10.8 us
    sub x1, other arithmetic, attend(): expo = jnp.exp(scores - top)  10.1 us
    all_to_all x1, waiting for transfers between devices, on_device(): lax.all_to_all(returned, 'seq', split_axis=0, concat_axis=0, tiled=True)  9.05 us
    all_to_all x1, starting transfers between devices, on_device(): lax.all_to_all(outgoing(k_all), 'seq', split_axis=0, concat_axis=0, tiled...  8.58 us
    all_to_all x1, waiting for transfers between devices, on_device(): lax.all_to_all(outgoing(v_all), 'seq', split_axis=0, concat_axis=0, tiled...  8.46 us
    all_to_all x1, starting transfers between devices, on_device(): lax.all_to_all(outgoing(q_all), 'seq', split_axis=0, concat_axis=0, tiled...  7.38 us
  transfers between devices with their start and end apart: 4, of which 3 were waited for; matrix products, arithmetic and copies ran while one was open for 32% of the time, Pallas kernels for 0%

commit v1 on v0

v1 whole, which is shorter than its diff:
```python
import functools

import jax
import jax.numpy as jnp
from jax import lax
from jax.experimental import pallas as pl
from jax.experimental.pallas import tpu as pltpu
from jax.sharding import PartitionSpec as P

HEADS = 40
HD = 128
TEMPORAL = 4
BLK = 64
PG = 8
NEG = -1e30
LOG2E = 1.4426950408889634
SCALE = HD**-0.5 * LOG2E


def attend(query, key, value, bias):
    scores = lax.dot_general(
        query, key, (((1,), (1,)), ((), ())), preferred_element_type=jnp.float32
    )
    scores = scores + bias
    top = jnp.max(scores, axis=1, keepdims=True)
    expo = jnp.exp2((scores - top) * SCALE).astype(jnp.bfloat16)
    wide = jnp.concatenate([value, jnp.ones_like(value)], axis=1)
    mixed = jnp.dot(expo, wide, preferred_element_type=jnp.float32)
    return (mixed[:, :HD] / mixed[:, HD:]).astype(jnp.bfloat16)


def kernel(
    n,
    heads_hbm,
    smask_hbm,
    tmask_hbm,
    q_hbm,
    k_hbm,
    v_hbm,
    out,
    heads,
    smask,
    tmask,
    q,
    k,
    v,
    sbias,
    tbias,
    send,
    recv,
    osend,
    orecv,
    load_sem,
    small_sem,
    send_sem,
    recv_sem,
    osend_sem,
    orecv_sem,
):
    me = lax.axis_index("seq")
    tok = q.shape[1]

    def peer_of(step):
        return lax.rem(me + step, n)

    barrier = pltpu.get_barrier_semaphore()

    @pl.loop(1, n)
    def _(step):
        pl.semaphore_signal(barrier, inc=1, device_id={"seq": peer_of(step)})

    small = [
        pltpu.make_async_copy(heads_hbm, heads, small_sem.at[0]),
        pltpu.make_async_copy(smask_hbm, smask, small_sem.at[1]),
        pltpu.make_async_copy(tmask_hbm, tmask, small_sem.at[2]),
    ]
    small[0].start()
    for part, (src, dst) in enumerate(((q_hbm, q), (k_hbm, k), (v_hbm, v))):

        @pl.loop(0, HEADS)
        def _(h):
            column = pl.ds(pl.multiple_of(h * HD, HD), HD)
            pltpu.make_async_copy(src.at[:, column], dst.at[h], load_sem.at[part]).start()

    small[1].start()
    small[2].start()

    small[0].wait()
    for part, ref in enumerate((q, k, v)):
        pltpu.make_async_copy(ref, ref, load_sem.at[part]).wait()
        for i in range(TEMPORAL):
            send[i, :, part] = ref[heads[i]].reshape(n, PG, HD)

    small[1].wait()
    small[2].wait()
    blocks = tok // BLK
    for i in range(blocks):
        for j in range(blocks):
            one = jnp.float32(0.0) if i == j else jnp.where(smask[0, i, j] != 0, 0.0, NEG)
            sbias[pl.ds(i * BLK, BLK), pl.ds(j * BLK, BLK)] = jnp.full((BLK, BLK), one, jnp.float32)
    allow = (tmask[...] != 0).astype(jnp.float32)
    rows = lax.broadcasted_iota(jnp.int32, (tok, n), 0) // PG
    cols = lax.broadcasted_iota(jnp.int32, (tok, n), 1)
    spread = (rows == cols).astype(jnp.float32)
    wide = jnp.dot(spread, allow, preferred_element_type=jnp.float32)
    wide = lax.dot_general(
        wide, spread, (((1,), (1,)), ((), ())), preferred_element_type=jnp.float32
    )
    same = (
        lax.broadcasted_iota(jnp.int32, (tok, tok), 0) // PG
        == lax.broadcasted_iota(jnp.int32, (tok, tok), 1) // PG
    )
    tbias[...] = jnp.where((wide > 0.5) | same, 0.0, NEG)

    pl.semaphore_wait(barrier, n - 1)

    for i in range(TEMPORAL):

        @pl.loop(1, n)
        def _(step):
            peer = peer_of(step)
            pltpu.make_async_remote_copy(
                src_ref=send.at[i, peer],
                dst_ref=recv.at[i, me],
                send_sem=send_sem.at[i],
                recv_sem=recv_sem.at[i],
                device_id={"seq": peer},
            ).start()

        pltpu.make_async_copy(send.at[i, me], recv.at[i, me], recv_sem.at[i]).start()

    def spatial(first, last):
        @pl.loop(first, last)
        def _(h):
            column = pl.ds(pl.multiple_of(h * HD, HD), HD)
            out[:, column] = attend(q[h], k[h], v[h], sbias[...])

    cuts = (0, 20, 27, 34, 40)
    for i in range(TEMPORAL):
        spatial(cuts[i], cuts[i + 1])
        pltpu.make_async_copy(recv.at[i], recv.at[i], recv_sem.at[i]).wait()
        mixed = attend(
            recv[i, :, 0].reshape(tok, HD),
            recv[i, :, 1].reshape(tok, HD),
            recv[i, :, 2].reshape(tok, HD),
            tbias[...],
        )
        osend[i] = mixed.reshape(n, PG, HD)

        @pl.loop(1, n)
        def _(step):
            peer = peer_of(step)
            pltpu.make_async_remote_copy(
                src_ref=osend.at[i, peer],
                dst_ref=orecv.at[i, me],
                send_sem=osend_sem.at[i],
                recv_sem=orecv_sem.at[i],
                device_id={"seq": peer},
            ).start()

        pltpu.make_async_copy(osend.at[i, me], orecv.at[i, me], orecv_sem.at[i]).start()

    for i in range(TEMPORAL):
        pltpu.make_async_copy(orecv.at[i], orecv.at[i], orecv_sem.at[i]).wait()

    @pl.loop(0, HEADS)
    def _(h):
        column = pl.ds(pl.multiple_of(h * HD, HD), HD)
        slot = jnp.int32(0)
        hit = jnp.int32(0)
        for i in range(TEMPORAL):
            match = heads[i] == h
            slot = jnp.where(match, i, slot)
            hit = jnp.where(match, 1, hit)
        moved = orecv[slot].reshape(tok, HD)
        out[:, column] = jnp.where(hit != 0, moved, out[:, column])

    for i in range(TEMPORAL):
        some = pl.ds(0, n - 1)
        pltpu.make_async_copy(send.at[i, some], send.at[i, some], send_sem.at[i]).wait()
        pltpu.make_async_copy(osend.at[i, some], osend.at[i, some], osend_sem.at[i]).wait()


def on_device(queries, keys, values, temporal_heads, spatial_mask, temporal_mask):
    n = lax.axis_size("seq")
    tok, width = queries.shape
    bf16 = jnp.bfloat16
    anywhere = pl.BlockSpec(memory_space=pltpu.HBM)
    return pl.pallas_call(
        functools.partial(kernel, n),
        out_shape=jax.ShapeDtypeStruct((tok, width), bf16),
        in_specs=[anywhere] * 6,
        out_specs=pl.BlockSpec(memory_space=pltpu.VMEM),
        scratch_shapes=[
            pltpu.SMEM((TEMPORAL,), jnp.int32),
            pltpu.SMEM(spatial_mask.shape, jnp.int32),
            pltpu.VMEM(temporal_mask.shape, jnp.int32),
            pltpu.VMEM((HEADS, tok, HD), bf16),
            pltpu.VMEM((HEADS, tok, HD), bf16),
            pltpu.VMEM((HEADS, tok, HD), bf16),
            pltpu.VMEM((tok, tok), jnp.float32),
            pltpu.VMEM((tok, tok), jnp.float32),
            pltpu.VMEM((TEMPORAL, n, 3, PG, HD), bf16),
            pltpu.VMEM((TEMPORAL, n, 3, PG, HD), bf16),
            pltpu.VMEM((TEMPORAL, n, PG, HD), bf16),
            pltpu.VMEM((TEMPORAL, n, PG, HD), bf16),
            pltpu.SemaphoreType.DMA((3,)),
            pltpu.SemaphoreType.DMA((3,)),
            pltpu.SemaphoreType.DMA((TEMPORAL,)),
            pltpu.SemaphoreType.DMA((TEMPORAL,)),
            pltpu.SemaphoreType.DMA((TEMPORAL,)),
            pltpu.SemaphoreType.DMA((TEMPORAL,)),
        ],
        compiler_params=pltpu.CompilerParams(
            collective_id=0, has_side_effects=True, vmem_limit_bytes=48 << 20
        ),
    )(temporal_heads, spatial_mask, temporal_mask, queries, keys, values)


def solution(mesh):
    placed = (
        P(("video", "seq"), None),
        P(("video", "seq"), None),
        P(("video", "seq"), None),
        P(),
        P("seq", None, None),
        P(),
    )
    return jax.shard_map(
        on_device, mesh=mesh, in_specs=placed, out_specs=P(("video", "seq"), None), check_vma=False
    )
```

time: 132 us -> 41.6 us (0.32)
  local copies, waits for them, and re-layouts: 53.3 us -> 5.29 us
  Pallas kernels: 0 us -> 36.1 us
  starting transfers between devices: 24.5 us -> 0 us
  other arithmetic: 24.4 us -> 0 us
  waiting for transfers between devices: 20 us -> 0 us
  matrix products: 8.21 us -> 0 us
    pallas_call x0 -> x1, Pallas kernels: none -> 36.1 us  [on_device(): pl.pallas_call(functools.partial(kernel, n), out_shape=jax.ShapeDtypeStru...]
    all_to_all x4 -> x0, starting transfers between devices: 24.5 us -> none  [the longest x1 8.58 us: on_device(): lax.all_to_all(outgoing(k_all), 'seq', split_axis=0, concat_axis=0, tiled...]
    all_to_all x4 -> x0, waiting for transfers between devices: 20 us -> none  [the longest x1 9.05 us: on_device(): lax.all_to_all(returned, 'seq', split_axis=0, concat_axis=0, tiled=True)]
    reshape x10 -> x0, local copies, waits for them, and re-layouts: 17 us -> none  [the longest x3 10.8 us: arrange(): return jnp.take(array.reshape(tok_rows, HEADS, HD), order, axis=1)]
    gather x5 -> x0, local copies, waits for them, and re-layouts: 14.9 us -> none  [the longest x4 12.5 us: arrange(): return jnp.take(array.reshape(tok_rows, HEADS, HD), order, axis=1)]
    unnamed x17 -> x9, local copies, waits for them, and re-layouts: 16.4 us -> 5.29 us
    sub x1 -> x0, other arithmetic: 10.1 us -> none  [attend(): expo = jnp.exp(scores - top)]
    dot_general x3 -> x0, matrix products: 7.71 us -> none  [the longest x1 5.02 us: attend(): jnp.einsum('qhd,khd->hqk', query, key, preferred_element_type=jnp.float32)]
  transfers between devices with their start and end apart: 4 -> 0, of which waited for: 3 -> 0; matrix products, arithmetic and copies ran while one was open for 32% -> 0% of each run, Pallas kernels for 0% -> 0%
where the time goes in v1:
time: 41.6 us; the launch traced here: 41.4 us
  Pallas kernels  36.1 us (87%)
  local copies, waits for them, and re-layouts  5.29 us (13%)
    pallas_call x1, Pallas kernels, on_device(): pl.pallas_call(functools.partial(kernel, n), out_shape=jax.ShapeDtypeStru...  36.1 us
    unnamed x9, local copies, waits for them, and re-layouts  5.29 us

profile of v1, /device:TPU:1, one launch (start us, length us, event | category | flops | bytes accessed | tf_op | source)
XLA Modules:
  0.0 41.4 jit_solution(1397306705413288626)
XLA Ops:
  0.0 0.0 copy-start
  0.0 1.7 %copy-done = bf16[256,5120]{1,0:T(8,128)(2,1)S(1)} copy-done((bf16[256,5120]{1,0:T(8,128)(2,1)S(1)}, bf16[256,5120]{1,0:T(8,128)(2,1)}, u32[]{:S(2)}) %copy-start) | copy-done | bytes 2621464
  1.7 0.0 copy-start.1
  1.7 0.7 %copy-done.1 = s32[32,32]{1,0:T(8,128)S(1)} copy-done((s32[32,32]{1,0:T(8,128)S(1)}, s32[32,32]{1,0:T(8,128)}, u32[]{:S(2)}) %copy-start.1) | copy-done | bytes 4120
  2.5 0.0 copy-start.2
  2.5 0.7 %copy-done.2 = s32[1,4,4]{2,1,0:T(4,128)S(1)} copy-done((s32[1,4,4]{2,1,0:T(4,128)S(1)}, s32[1,4,4]{2,1,0:T(4,128)}, u32[]{:S(2)}) %copy-start.2) | copy-done | bytes 88
  3.1 0.0 copy-start.3
  3.1 0.7 %copy-done.3 = s32[4]{0:T(128)S(1)} copy-done((s32[4]{0:T(128)S(1)}, s32[4]{0:T(128)}, u32[]{:S(2)}) %copy-start.3) | copy-done | bytes 40
  3.8 36.1 %shard_map.64 = bf16[256,5120]{1,0:T(8,128)(2,1)S(1)} custom-call(s32[4]{0:T(128)S(1)} %copy-done.3, s32[1,4,4]{2,1,0:T(4,128)S(1)} %copy-done.2, s32[32,32]{1,0:T(8,128)S(1)} %copy-done.1, bf16[256,5120]{1,0:T(8,128)(2,1)S(1)} %copy-done, bf16[256,5120]{1,0:T(8,128)(2,1)} %k_hbm.1, bf16[256,5120]{1,0:T(8,128)(2,1)} %v_hbm.1), custom_call_target="tpu_custom_call" | custom-call | tf_op jit(solution)/shard_map/pallas_call | solution.py:189
  39.9 1.5 %copy.8 = bf16[256,5120]{1,0:T(8,128)(2,1)} copy(bf16[256,5120]{1,0:T(8,128)(2,1)S(1)} %shard_map.64) | data formatting | bytes 5242880
Async XLA Ops:
  0.0 1.7 %copy-start = (bf16[256,5120]{1,0:T(8,128)(2,1)S(1)}, bf16[256,5120]{1,0:T(8,128)(2,1)}, u32[]{:S(2)}) copy-start(bf16[256,5120]{1,0:T(8,128)(2,1)} %q_hbm.1) | copy-start | bytes 7864324
  1.7 0.7 %copy-start.1 = (s32[32,32]{1,0:T(8,128)S(1)}, s32[32,32]{1,0:T(8,128)}, u32[]{:S(2)}) copy-start(s32[32,32]{1,0:T(8,128)} %tmask_hbm.1) | copy-start | bytes 12292
  2.5 0.7 %copy-start.2 = (s32[1,4,4]{2,1,0:T(4,128)S(1)}, s32[1,4,4]{2,1,0:T(4,128)}, u32[]{:S(2)}) copy-start(s32[1,4,4]{2,1,0:T(4,128)} %smask_hbm.1) | copy-start | bytes 196
  3.1 0.7 %copy-start.3 = (s32[4]{0:T(128)S(1)}, s32[4]{0:T(128)}, u32[]{:S(2)}) copy-start(s32[4]{0:T(128)} %heads_hbm.1) | copy-start | bytes 52

commit v2 on v1

v2 whole, which is shorter than its diff:
```python
import functools

import jax
import jax.numpy as jnp
from jax import lax
from jax.experimental import pallas as pl
from jax.experimental.pallas import tpu as pltpu
from jax.sharding import PartitionSpec as P

HEADS = 40
HD = 128
TEMPORAL = 4
BLK = 64
PG = 8
NEG = -1e30
LOG2E = 1.4426950408889634
SCALE = HD**-0.5 * LOG2E


SPATIAL = 36
UNROLL = 6
SEGMENTS = (0, 18, 24, 30, 36)
STAGES = (3, 0, 1, 2)


def score(query, key, bias):
    return (
        lax.dot_general(query, key, (((1,), (1,)), ((), ())), preferred_element_type=jnp.float32)
        + bias
    )


def weigh(scores):
    top = jnp.max(scores, axis=1, keepdims=True)
    return jnp.exp2((scores - top) * SCALE).astype(jnp.bfloat16)


def mix(expo, value):
    wide = jnp.concatenate([value, jnp.ones_like(value)], axis=1)
    mixed = jnp.dot(expo, wide, preferred_element_type=jnp.float32)
    return (mixed[:, :HD] / mixed[:, HD:]).astype(jnp.bfloat16)


def attention_kernel(
    n,
    heads_hbm,
    smask_hbm,
    tmask_hbm,
    q_hbm,
    k_hbm,
    v_hbm,
    spatial_out,
    orecv,
    heads,
    smask,
    tmask,
    q,
    k,
    v,
    sbias,
    tbias,
    scores,
    expos,
    send,
    recv,
    osend,
    first_sem,
    load_sem,
    small_sem,
    send_sem,
    recv_sem,
    osend_sem,
    orecv_sem,
):
    me = lax.axis_index("seq")
    tok = q.shape[1]

    def peer_of(step):
        return lax.rem(me + step, n)

    barrier = pltpu.get_barrier_semaphore()

    @pl.loop(1, n)
    def _(step):
        pl.semaphore_signal(barrier, inc=1, device_id={"seq": peer_of(step)})

    pairs = ((q_hbm, q), (k_hbm, k), (v_hbm, v))
    last = HEADS - 1
    first = [
        pltpu.make_async_copy(src.at[:, pl.ds(last * HD, HD)], dst.at[last], first_sem.at[part])
        for part, (src, dst) in enumerate(pairs)
    ]
    for copy in first:
        copy.start()
    small = [
        pltpu.make_async_copy(heads_hbm, heads, small_sem.at[0]),
        pltpu.make_async_copy(smask_hbm, smask, small_sem.at[1]),
        pltpu.make_async_copy(tmask_hbm, tmask, small_sem.at[2]),
    ]
    for copy in small:
        copy.start()
    for part, (src, dst) in enumerate(pairs):

        @pl.loop(0, last)
        def _(h):
            column = pl.ds(pl.multiple_of(h * HD, HD), HD)
            pltpu.make_async_copy(src.at[:, column], dst.at[h], load_sem.at[part]).start()

    for part, ref in enumerate((q, k, v)):
        first[part].wait()
        send[TEMPORAL - 1, :, part] = ref[last].reshape(n, PG, HD)

    small[1].wait()
    small[2].wait()
    blocks = tok // BLK
    for i in range(blocks):
        for j in range(blocks):
            one = jnp.float32(0.0) if i == j else jnp.where(smask[0, i, j] != 0, 0.0, NEG)
            sbias[pl.ds(i * BLK, BLK), pl.ds(j * BLK, BLK)] = jnp.full((BLK, BLK), one, jnp.float32)
    allow = (tmask[...] != 0).astype(jnp.float32)
    rows = lax.broadcasted_iota(jnp.int32, (tok, n), 0) // PG
    cols = lax.broadcasted_iota(jnp.int32, (tok, n), 1)
    spread = (rows == cols).astype(jnp.float32)
    wide = jnp.dot(spread, allow, preferred_element_type=jnp.float32)
    wide = lax.dot_general(
        wide, spread, (((1,), (1,)), ((), ())), preferred_element_type=jnp.float32
    )
    same = (
        lax.broadcasted_iota(jnp.int32, (tok, tok), 0) // PG
        == lax.broadcasted_iota(jnp.int32, (tok, tok), 1) // PG
    )
    tbias[...] = jnp.where((wide > 0.5) | same, 0.0, NEG)

    def scatter(src, dst, src_sem, dst_sem):
        @pl.loop(1, n)
        def _(step):
            peer = peer_of(step)
            pltpu.make_async_remote_copy(
                src_ref=src.at[peer],
                dst_ref=dst.at[me],
                send_sem=src_sem,
                recv_sem=dst_sem,
                device_id={"seq": peer},
            ).start()

        pltpu.make_async_copy(src.at[me], dst.at[me], dst_sem).start()

    pl.semaphore_wait(barrier, n - 1)
    for i in STAGES[:1]:
        scatter(send.at[i], recv.at[i], send_sem.at[i], recv_sem.at[i])
    small[0].wait()
    for part, ref in enumerate((q, k, v)):
        rest = ref.at[pl.ds(0, last)]
        pltpu.make_async_copy(rest, rest, load_sem.at[part]).wait()
        for i in STAGES[1:]:
            send[i, :, part] = ref[heads[i]].reshape(n, PG, HD)
    for i in STAGES[1:]:
        scatter(send.at[i], recv.at[i], send_sem.at[i], recv_sem.at[i])

    def head_of(j):
        h = jnp.minimum(j, SPATIAL - 1)
        for i in range(TEMPORAL):
            h = h + jnp.where(heads[i] <= h, 1, 0)
        return h

    def ahead(j, slot):
        h = head_of(j)
        scores[slot] = score(q[h], k[h], sbias[...])

    ahead(0, 0)
    ahead(1, 1)
    expos[0] = weigh(scores[0])

    for stage, i in enumerate(STAGES):

        @pl.loop(SEGMENTS[stage], SEGMENTS[stage + 1], step=UNROLL)
        def _(base):
            for step in range(UNROLL):
                slot = step % 2
                ahead(base + step + 2, slot)
                expos[1 - slot] = weigh(scores[1 - slot])
                spatial_out[base + step] = mix(expos[slot], v[head_of(base + step)])

        pltpu.make_async_copy(recv.at[i], recv.at[i], recv_sem.at[i]).wait()
        got = [recv[i, :, part].reshape(tok, HD) for part in range(3)]
        mixed = mix(weigh(score(got[0], got[1], tbias[...])), got[2])
        osend[i] = mixed.reshape(n, PG, HD)
        scatter(osend.at[i], orecv.at[i], osend_sem.at[i], orecv_sem.at[i])

    for i in STAGES:
        pltpu.make_async_copy(orecv.at[i], orecv.at[i], orecv_sem.at[i]).wait()
    for i in STAGES:
        some = pl.ds(0, n - 1)
        pltpu.make_async_copy(send.at[i, some], send.at[i, some], send_sem.at[i]).wait()
        pltpu.make_async_copy(osend.at[i, some], osend.at[i, some], osend_sem.at[i]).wait()


def place_kernel(heads, spatial, temporal, out, sem):
    @pl.loop(0, SPATIAL)
    def _(j):
        h = j
        for i in range(TEMPORAL):
            h = h + jnp.where(heads[i] <= h, 1, 0)
        column = pl.ds(pl.multiple_of(h * HD, HD), HD)
        pltpu.make_async_copy(spatial.at[j], out.at[:, column], sem).start()

    for i in range(TEMPORAL):
        column = pl.ds(pl.multiple_of(heads[i] * HD, HD), HD)
        pltpu.make_async_copy(temporal.at[i], out.at[:, column], sem).start()
    pltpu.make_async_copy(out, out, sem).wait()


def on_device(queries, keys, values, temporal_heads, spatial_mask, temporal_mask):
    n = lax.axis_size("seq")
    tok, width = queries.shape
    bf16 = jnp.bfloat16
    operands = (temporal_heads, spatial_mask, temporal_mask, queries, keys, values)
    in_vmem = pl.BlockSpec(memory_space=pltpu.VMEM)
    in_hbm = pl.BlockSpec(memory_space=pltpu.HBM)
    spatial, temporal = pl.pallas_call(
        functools.partial(attention_kernel, n),
        out_shape=(
            pltpu.VMEM((SPATIAL, tok, HD), bf16),
            pltpu.VMEM((TEMPORAL, n, PG, HD), bf16),
        ),
        in_specs=[in_hbm] * 6,
        out_specs=(in_vmem, in_vmem),
        scratch_shapes=[
            pltpu.SMEM((TEMPORAL,), jnp.int32),
            pltpu.SMEM(spatial_mask.shape, jnp.int32),
            pltpu.VMEM(temporal_mask.shape, jnp.int32),
            pltpu.VMEM((HEADS, tok, HD), bf16),
            pltpu.VMEM((HEADS, tok, HD), bf16),
            pltpu.VMEM((HEADS, tok, HD), bf16),
            pltpu.VMEM((tok, tok), jnp.float32),
            pltpu.VMEM((tok, tok), jnp.float32),
            pltpu.VMEM((2, tok, tok), jnp.float32),
            pltpu.VMEM((2, tok, tok), bf16),
            pltpu.VMEM((TEMPORAL, n, 3, PG, HD), bf16),
            pltpu.VMEM((TEMPORAL, n, 3, PG, HD), bf16),
            pltpu.VMEM((TEMPORAL, n, PG, HD), bf16),
            pltpu.SemaphoreType.DMA((3,)),
            pltpu.SemaphoreType.DMA((3,)),
            pltpu.SemaphoreType.DMA((3,)),
            pltpu.SemaphoreType.DMA((TEMPORAL,)),
            pltpu.SemaphoreType.DMA((TEMPORAL,)),
            pltpu.SemaphoreType.DMA((TEMPORAL,)),
            pltpu.SemaphoreType.DMA((TEMPORAL,)),
        ],
        compiler_params=pltpu.CompilerParams(
            collective_id=0, has_side_effects=True, vmem_limit_bytes=48 << 20
        ),
    )(*[pltpu.with_memory_space_constraint(x, pltpu.HBM) for x in operands])
    temporal = temporal.reshape(TEMPORAL, tok, HD)
    return pl.pallas_call(
        place_kernel,
        out_shape=jax.ShapeDtypeStruct((tok, width), bf16),
        in_specs=[pl.BlockSpec(memory_space=pltpu.SMEM), in_vmem, in_vmem],
        out_specs=in_hbm,
        scratch_shapes=[pltpu.SemaphoreType.DMA],
        compiler_params=pltpu.CompilerParams(vmem_limit_bytes=8 << 20),
    )(temporal_heads, spatial, temporal)


def solution(mesh):
    placed = (
        P(("video", "seq"), None),
        P(("video", "seq"), None),
        P(("video", "seq"), None),
        P(),
        P("seq", None, None),
        P(),
    )
    return jax.shard_map(
        on_device, mesh=mesh, in_specs=placed, out_specs=P(("video", "seq"), None), check_vma=False
    )
```

time: 41.6 us -> 27 us (0.65)
  Pallas kernels: 36.1 us -> 26.9 us
  local copies, waits for them, and re-layouts: 5.29 us -> 0.01 us
    pallas_call x1 -> x2, Pallas kernels: 36.1 us -> 26.9 us  [the longest x1 24.9 us: on_device(): pl.pallas_call(functools.partial(attention_kernel, n), out_shape=(pltpu.V...]
    unnamed x9 -> x2, local copies, waits for them, and re-layouts: 5.29 us -> 0.01 us
where the time goes in v2:
time: 27 us; the launch traced here: 26.9 us
  Pallas kernels  26.9 us (100%)
    pallas_call x1, Pallas kernels, on_device(): pl.pallas_call(functools.partial(attention_kernel, n), out_shape=(pltpu.V...  24.9 us
    pallas_call x1, Pallas kernels, on_device(): pl.pallas_call(place_kernel, out_shape=jax.ShapeDtypeStruct((tok, width),...  2.02 us

profile of v2, /device:TPU:1, one launch (start us, length us, event | category | flops | bytes accessed | tf_op | source)
XLA Modules:
  0.0 26.9 jit_solution(14363439924008517646)
XLA Ops:
  0.0 0.0 copy-start
  0.0 24.9 %shard_map.64 = (bf16[36,256,128]{2,1,0:T(8,128)(2,1)S(1)}, bf16[4,32,8,128]{3,2,1,0:T(8,128)(2,1)S(1)}) custom-call(s32[4]{0:T(128)} %heads.1, s32[1,4,4]{2,1,0:T(4,128)} %smask_hbm.1, s32[32,32]{1,0:T(8,128)} %tmask_hbm.1, bf16[256,5120]{1,0:T(8,128)(2,1)} %q_hbm.1, bf16[256,5120]{1,0:T(8,128)(2,1)} %k_hbm.1, bf16[256,5120]{1,0:T(8,128)(2,1)} %v_hbm.1), custom_call_target="tpu_custom_call" | custom-call | tf_op jit(solution)/shard_map/pallas_call | solution.py:220
  24.9 0.0 copy-done
  24.9 2.0 %shard_map.65 = bf16[256,5120]{1,0:T(8,128)(2,1)} custom-call(s32[4]{0:T(128)S(1)} %copy-done, bf16[36,256,128]{2,1,0:T(8,128)(2,1)S(1)} %get-tuple-element.7.spatial, bf16[4,256,128]{2,1,0:T(8,128)(2,1)S(1)} %bitcast.1), custom_call_target="tpu_custom_call" | custom-call | tf_op jit(solution)/shard_map/pallas_call | solution.py:255
Async XLA Ops:
  0.0 24.9 %copy-start = (s32[4]{0:T(128)S(1)}, s32[4]{0:T(128)}, u32[]{:S(2)}) copy-start(s32[4]{0:T(128)} %heads.1) | copy-start | bytes 52

commit v3 on v2

--- a/solution.py
+++ b/solution.py
@@ -21,6 +21,10 @@
 UNROLL = 6
 SEGMENTS = (0, 18, 24, 30, 36)
 STAGES = (3, 0, 1, 2)
+FAR = (
+    (2, 2), (2, 1), (1, 2), (2, 3), (3, 2), (1, 1), (3, 3), (1, 3),
+    (3, 1), (2, 0), (0, 2), (1, 0), (0, 1), (3, 0), (0, 3),
+)
 
 
 def score(query, key, bias):
@@ -39,6 +43,13 @@
     wide = jnp.concatenate([value, jnp.ones_like(value)], axis=1)
     mixed = jnp.dot(expo, wide, preferred_element_type=jnp.float32)
     return (mixed[:, :HD] / mixed[:, HD:]).astype(jnp.bfloat16)
+
+
+def spread_head(j, heads):
+    h = j
+    for i in range(TEMPORAL):
+        h = h + jnp.where(heads[i] - i <= j, 1, 0)
+    return h
 
 
 def attention_kernel(
@@ -75,14 +86,15 @@
     me = lax.axis_index("seq")
     tok = q.shape[1]
 
-    def peer_of(step):
-        return lax.rem(me + step, n)
+    xs = [lax.rem(me // 8 + d, 4) * 8 for d in range(4)]
+    ys = [lax.rem(lax.rem(me // 2, 4) + d, 4) * 2 for d in range(4)]
+    cs = [lax.rem(me + d, 2) for d in range(2)]
+    peers = [xs[dx] + ys[dy] + cs[dc] for dx, dy in FAR for dc in range(2)]
+    peers.append(xs[0] + ys[0] + cs[1])
 
     barrier = pltpu.get_barrier_semaphore()
-
-    @pl.loop(1, n)
-    def _(step):
-        pl.semaphore_signal(barrier, inc=1, device_id={"seq": peer_of(step)})
+    for peer in peers:
+        pl.semaphore_signal(barrier, inc=1, device_id={"seq": peer})
 
     pairs = ((q_hbm, q), (k_hbm, k), (v_hbm, v))
     last = HEADS - 1
@@ -110,6 +122,22 @@
         first[part].wait()
         send[TEMPORAL - 1, :, part] = ref[last].reshape(n, PG, HD)
 
+    def scatter(src, dst, src_sem, dst_sem):
+        for peer in peers:
+            pltpu.make_async_remote_copy(
+                src_ref=src.at[peer],
+                dst_ref=dst.at[me],
+                send_sem=src_sem,
+                recv_sem=dst_sem,
+                device_id={"seq": peer},
+            ).start()
+
+        pltpu.make_async_copy(src.at[me], dst.at[me], dst_sem).start()
+
+    pl.semaphore_wait(barrier, n - 1)
+    for i in STAGES[:1]:
+        scatter(send.at[i], recv.at[i], send_sem.at[i], recv_sem.at[i])
+
     small[1].wait()
     small[2].wait()
     blocks = tok // BLK
@@ -131,23 +159,6 @@
     )
     tbias[...] = jnp.where((wide > 0.5) | same, 0.0, NEG)
 
-    def scatter(src, dst, src_sem, dst_sem):
-        @pl.loop(1, n)
-        def _(step):
-            peer = peer_of(step)
-            pltpu.make_async_remote_copy(
-                src_ref=src.at[peer],
-                dst_ref=dst.at[me],
-                send_sem=src_sem,
-                recv_sem=dst_sem,
-                device_id={"seq": peer},
-            ).start()
-
-        pltpu.make_async_copy(src.at[me], dst.at[me], dst_sem).start()
-
-    pl.semaphore_wait(barrier, n - 1)
-    for i in STAGES[:1]:
-        scatter(send.at[i], recv.at[i], send_sem.at[i], recv_sem.at[i])
     small[0].wait()
     for part, ref in enumerate((q, k, v)):
         rest = ref.at[pl.ds(0, last)]
@@ -158,10 +169,7 @@
         scatter(send.at[i], recv.at[i], send_sem.at[i], recv_sem.at[i])
 
     def head_of(j):
-        h = jnp.minimum(j, SPATIAL - 1)
-        for i in range(TEMPORAL):
-            h = h + jnp.where(heads[i] <= h, 1, 0)
-        return h
+        return spread_head(jnp.minimum(j, SPATIAL - 1), heads)
 
     def ahead(j, slot):
         h = head_of(j)
@@ -196,16 +204,12 @@
 
 
 def place_kernel(heads, spatial, temporal, out, sem):
-    @pl.loop(0, SPATIAL)
-    def _(j):
-        h = j
-        for i in range(TEMPORAL):
-            h = h + jnp.where(heads[i] <= h, 1, 0)
-        column = pl.ds(pl.multiple_of(h * HD, HD), HD)
+    where = [heads[i] for i in range(TEMPORAL)]
+    for j in range(SPATIAL):
+        column = pl.ds(pl.multiple_of(spread_head(j, where) * HD, HD), HD)
         pltpu.make_async_copy(spatial.at[j], out.at[:, column], sem).start()
-
     for i in range(TEMPORAL):
-        column = pl.ds(pl.multiple_of(heads[i] * HD, HD), HD)
+        column = pl.ds(pl.multiple_of(where[i] * HD, HD), HD)
         pltpu.make_async_copy(temporal.at[i], out.at[:, column], sem).start()
     pltpu.make_async_copy(out, out, sem).wait()
 

time: 27 us -> 25.5 us (0.944)
  Pallas kernels: 26.9 us -> 25.4 us
    pallas_call x1, Pallas kernels: 24.9 us -> 23.4 us  [on_device(): pl.pallas_call(functools.partial(attention_kernel, n), out_shape=(pltpu.V...]
where the time goes in v3:
time: 25.5 us
  Pallas kernels  25.4 us (100%)
    pallas_call x1, Pallas kernels, on_device(): pl.pallas_call(functools.partial(attention_kernel, n), out_shape=(pltpu.V...  23.4 us
    pallas_call x1, Pallas kernels, on_device(): pl.pallas_call(place_kernel, out_shape=jax.ShapeDtypeStruct((tok, width),...  2.01 us

profile of v3, /device:TPU:1, one launch (start us, length us, event | category | flops | bytes accessed | tf_op | source)
XLA Modules:
  0.0 25.5 jit_solution(2909437755557036205)
XLA Ops:
  0.0 0.0 copy-start
  0.0 23.4 %shard_map.64 = (bf16[36,256,128]{2,1,0:T(8,128)(2,1)S(1)}, bf16[4,32,8,128]{3,2,1,0:T(8,128)(2,1)S(1)}) custom-call(s32[4]{0:T(128)} %heads.1, s32[1,4,4]{2,1,0:T(4,128)} %smask_hbm.1, s32[32,32]{1,0:T(8,128)} %tmask_hbm.1, bf16[256,5120]{1,0:T(8,128)(2,1)} %q_hbm.1, bf16[256,5120]{1,0:T(8,128)(2,1)} %k_hbm.1, bf16[256,5120]{1,0:T(8,128)(2,1)} %v_hbm.1), custom_call_target="tpu_custom_call" | custom-call | tf_op jit(solution)/shard_map/pallas_call | solution.py:224
  23.4 0.0 copy-done
  23.5 2.0 %shard_map.65 = bf16[256,5120]{1,0:T(8,128)(2,1)} custom-call(s32[4]{0:T(128)S(1)} %copy-done, bf16[36,256,128]{2,1,0:T(8,128)(2,1)S(1)} %get-tuple-element.7.spatial, bf16[4,256,128]{2,1,0:T(8,128)(2,1)S(1)} %bitcast.1), custom_call_target="tpu_custom_call" | custom-call | tf_op jit(solution)/shard_map/pallas_call | solution.py:259
Async XLA Ops:
  0.0 23.4 %copy-start = (s32[4]{0:T(128)S(1)}, s32[4]{0:T(128)}, u32[]{:S(2)}) copy-start(s32[4]{0:T(128)} %heads.1) | copy-start | bytes 52
